TPU v7x, 32 devices: a whole 2x2x4 slice. The times are simulated.
32 devices in a mesh: blk: 8 (over z, y), beam: 4 (over x, core).
Axes of the slice: x: 2, y: 2, z: 4, core: 2. Of those that a mesh axis runs over, the one named last changes fastest.
Arguments:
- signal: float32 [524288], P(('blk', 'beam')), may hold values from -6 to 6
- weight: float32 [524288], P(('blk', 'beam')), may hold values from 0.25 to 1
- cycle: int32 [524288], P(('blk', 'beam')), may hold values from 0 to 1
- phi: int32 [524288], P(('blk', 'beam')), may hold values from 0 to 2047
- psi: int32 [524288], P(('blk', 'beam')), may hold values from 0 to 31
- owner: int32 [4096, 1], P(('blk', 'beam')), may hold values from 0 to 7; in each aligned block of 128 rows (0 to 127, 128 to 255, ...) at most 40 rows name the same one
- wigner: bfloat16 [1024, 32, 16, 1152], P('blk', 'beam'), may hold values from -0.375 to 0.375
Outputs:
- alm: float32 [1024, 2, 1152], P(('blk', 'beam'))
Inputs may be any that keep to these rules, and one draw needn't show every extreme that they name: `owner`: among the 128 blocks of one device no cycle group is named by more than 40 blocks, and in some device's blocks one group is named by exactly 40.
All inputs are finite; a program needn't handle non-finite values.
Results may differ from a plain program's by a relative error of at most 0.02.
Values may be sent and summed in bfloat16 or wider, within the bound.
No kernel may reach another device: no remote copies, remote signals or barrier semaphores. Data moves between devices by JAX's collectives and lax.ppermute only.
A program may use at most 128 MiB of HBM per device.

v0:
```python
import math
import jax
import jax.numpy as jnp
from jax import lax
from jax.sharding import PartitionSpec as P

BLOCK_ROWS = 128
CYCLE_DEV = 2
NPSI = 32
NPHI = 2048


def psi_rows(psi_index, length):
    component = jnp.arange(length, dtype=jnp.int32)[:, None]
    middle = length // 2
    frequency = jnp.where(component <= middle, component, component - middle)
    residue = (frequency * psi_index[None, :] % length).astype(jnp.float32)
    angles = residue * jnp.float32(2.0 * math.pi / length)
    return jnp.where(component <= middle, jnp.cos(angles), jnp.sin(angles)) * jnp.float32(
        1.0 / math.sqrt(length)
    )


def phi_table(length):
    cell_index = jnp.arange(length, dtype=jnp.int32)[:, None]
    column = jnp.arange(length, dtype=jnp.int32)[None, :]
    residue = (column // 2 * cell_index % length).astype(jnp.float32)
    angles = residue * jnp.float32(2.0 * math.pi / length)
    values = jnp.where(column % 2 == 0, jnp.cos(angles), jnp.sin(angles)) * jnp.float32(
        1.0 / math.sqrt(length)
    )
    return values.astype(jnp.bfloat16)


def block_turns(total):
    turns = max(1, total // 2048)
    while total % turns != 0:
        turns = turns - 1
    return turns


def shards(signal, weight, cycle, phi, psi, owner, wigner):
    groups = lax.axis_size("blk")
    beams = lax.axis_size("beam")
    blocks = owner.shape[0]
    capacity = max(2, 5 * blocks // (2 * groups))
    slots = capacity * BLOCK_ROWS
    target_group = owner[:, 0]
    hits = (target_group[:, None] == jnp.arange(groups, dtype=jnp.int32)[None, :]).astype(jnp.int32)
    earlier = jnp.cumsum(hits, axis=0) - hits
    within = jnp.sum(earlier * hits, axis=1)
    position = target_group * capacity + within
    source = (
        jnp.zeros((groups * capacity,), jnp.int32)
        .at[position]
        .set(jnp.arange(blocks, dtype=jnp.int32))
    )
    filled = jnp.zeros((groups * capacity,), jnp.int32).at[position].set(1)

    def arrange(data):
        leading = data.shape[0]
        shaped = data.reshape(leading, blocks, BLOCK_ROWS)
        taken = jnp.take(shaped, source, axis=1)
        taken = jnp.where(filled[None, :, None] > 0, taken, jnp.zeros_like(taken))
        return taken.reshape(leading, groups, slots)

    sample_value = signal * weight
    packed = (cycle * NPSI + psi) * NPHI + phi
    total = groups * slots
    got_value, got_code = (
        lax.all_to_all(
            arrange(sample_value[None, :]).astype(jnp.bfloat16),
            "blk",
            split_axis=1,
            concat_axis=1,
            tiled=True,
        ).astype(jnp.float32),
        lax.all_to_all(arrange(packed[None, :]), "blk", split_axis=1, concat_axis=1, tiled=True),
    )
    codes = got_code.reshape(total)
    arrived = got_value.reshape(total)
    received = (psi_rows(codes // NPHI % NPSI, NPSI) * arrived[None, :]).astype(jnp.bfloat16)
    cycle_of = codes // (NPSI * NPHI)
    phi_of = codes % NPHI
    spread = jnp.concatenate(
        [
            jnp.where(cycle_of[None, :] == level, received, jnp.zeros_like(received))
            for level in range(CYCLE_DEV)
        ],
        axis=0,
    )
    turns = block_turns(total)
    width = total // turns
    columns = jnp.arange(NPHI, dtype=jnp.int32)

    def bin_block(number, carry):
        start = number * width
        part = lax.dynamic_slice_in_dim(spread, start, width, 1)
        place = lax.dynamic_slice_in_dim(phi_of, start, width, 0)
        onehot = (place[:, None] == columns[None, :]).astype(jnp.bfloat16)
        return carry + jnp.dot(part, onehot, preferred_element_type=jnp.float32)

    cube = lax.fori_loop(0, turns, bin_block, jnp.zeros((CYCLE_DEV * NPSI, NPHI), jnp.float32))
    cube = cube.reshape(CYCLE_DEV, NPSI, NPHI)
    share = NPSI // beams
    summed = lax.psum(cube.astype(jnp.bfloat16), "beam").astype(jnp.float32)
    mine = lax.dynamic_slice_in_dim(summed, lax.axis_index("beam") * share, share, 1)
    spectra = jnp.dot(
        mine.astype(jnp.bfloat16).reshape(CYCLE_DEV * share, NPHI),
        phi_table(NPHI),
        preferred_element_type=jnp.float32,
    )
    spectra = spectra.astype(jnp.bfloat16).reshape(CYCLE_DEV, share, NPHI)
    regrouped = lax.all_to_all(spectra, "blk", split_axis=2, concat_axis=0, tiled=True)
    orders = regrouped.shape[2] // 2
    coeffs = regrouped.reshape(regrouped.shape[0], share, orders, 2).transpose(2, 1, 0, 3)
    partial_sum = jnp.einsum("mqtl,mqtp->mpl", wigner, coeffs, preferred_element_type=jnp.float32)
    totals = lax.psum(partial_sum.astype(jnp.bfloat16), "beam").astype(jnp.float32)
    return lax.dynamic_slice_in_dim(
        totals, lax.axis_index("beam") * (orders // beams), orders // beams, 0
    )


def solution(mesh):
    return jax.shard_map(
        shards,
        mesh=mesh,
        in_specs=(
            P(("blk", "beam")),
            P(("blk", "beam")),
            P(("blk", "beam")),
            P(("blk", "beam")),
            P(("blk", "beam")),
            P(("blk", "beam"), None),
            P("blk", "beam", None, None),
        ),
        out_specs=P(("blk", "beam"), None, None),
        check_vma=False,
    )
```

profile of v0, /device:TPU:0, one launch (start us, length us, event | category | flops | bytes accessed | tf_op | source)
XLA Modules:
  0.0 333.1 jit_solution(5072294114963490575)
XLA Ops:
  16.1 7.3 %all-to-all-start.1 = ((bf16[8,2,2560]{2,1,0:T(2,128)(2,1)}), bf16[8,2,2560]{2,1,0:T(2,128)(2,1)S(1)}, u32[]{:S(2)}, u32[]{:S(2)}) async-start(bf16[8,2,2560]{2,1,0:T(2,128)(2,1)} %reshape.312), calls=%async_computation.1 | async-start | bytes 163840 | tf_op jit(solution)/shard_map/all_to_all | solution.py:71
  34.4 7.0 %all-to-all-done = s32[1,8,5120]{2,0,1:T(1,128)S(1)} async-done(((s32[1,8,5120]{2,0,1:T(1,128)}), s32[1,8,5120]{2,0,1:T(1,128)S(1)}, u32[]{:S(2)}, u32[]{:S(2)}) %all-to-all-start) | async-done | bytes 163872 | tf_op jit(solution)/shard_map/all_to_all | solution.py:78
  41.7 21.8 %broadcast_select_fusion.1 = (bf16[32,40960]{1,0:T(8,128)(2,1)S(1)}, bf16[32,40960]{1,0:T(8,128)(2,1)S(1)}) fusion(pred[40960]{0:T(1024)(128)(4,1)S(1)} %get-tuple-element.129, f32[40960]{0:T(1024)S(1)} %bitcast.53, s32[40960]{0:T(1024)S(1)} %get-tuple-element.128, s32[32]{0:T(128)S(1)} %add_select_fusion.8, pred[32]{0:T(512)(128)(4,1)S(1)} %iota_compare_fusion.5, ...), kind=kLoop, calls=%fused_computation.37 | loop fusion | flops 24903680 | bytes 5652640 | tf_op jit(solution)/shard_map/jit(_where)/select_n | solution.py:87
  66.2 90.4 %while.14 = (s32[]{:T(128)}, f32[64,2048]{1,0:T(8,128)S(1)}, bf16[64,40960]{1,0:T(8,128)(2,1)}, s32[40960]{0:T(1024)S(1)}, s32[]{:T(128)}, /*index=5*/s32[]{:T(128)}, s32[]{:T(128)}, s32[]{:T(128)}) while((s32[]{:T(128)}, f32[64,2048]{1,0:T(8,128)S(1)}, bf16[64,40960]{1,0:T(8,128)(2,1)}, s32[40960]{0:T(1024)S(1)}, s32[]{:T(128)}, ...), condition=%wide.region_5.6_spmd.clone, body=%wide.region_4.5_spmd.clone.sunk | while | flops 541327360 | bytes 1335445 | solution.py:103
  70.7 4.5 %fusion.59 = f32[64,2048]{1,0:T(8,128)S(1)} fusion(s32[2048]{0:T(1024)S(1)} %dynamic_slice.39, f32[64,2048]{1,0:T(8,128)S(1)} %get-tuple-element.165, bf16[64,40960]{1,0:T(8,128)(2,1)} %get-tuple-element.174, s32[]{:T(128)S(6)} %select_n.263, pred[]{:T(512)S(6)} %compare.34), kind=kOutput, calls=%fused_computation.8.clone.1 | convolution fusion | flops 541327360 | bytes 1318917 | tf_op jit(solution)/shard_map/while/body/eval_jaxpr/dot_general | solution.py:101
  75.3 4.5 %fusion.59 = f32[64,2048]{1,0:T(8,128)S(1)} fusion(s32[2048]{0:T(1024)S(1)} %dynamic_slice.39, f32[64,2048]{1,0:T(8,128)S(1)} %get-tuple-element.165, bf16[64,40960]{1,0:T(8,128)(2,1)} %get-tuple-element.174, s32[]{:T(128)S(6)} %select_n.263, pred[]{:T(512)S(6)} %compare.34), kind=kOutput, calls=%fused_computation.8.clone.1 | convolution fusion | flops 541327360 | bytes 1318917 | tf_op jit(solution)/shard_map/while/body/eval_jaxpr/dot_general | solution.py:101
  79.8 4.5 %fusion.59 = f32[64,2048]{1,0:T(8,128)S(1)} fusion(s32[2048]{0:T(1024)S(1)} %dynamic_slice.39, f32[64,2048]{1,0:T(8,128)S(1)} %get-tuple-element.165, bf16[64,40960]{1,0:T(8,128)(2,1)} %get-tuple-element.174, s32[]{:T(128)S(6)} %select_n.263, pred[]{:T(512)S(6)} %compare.34), kind=kOutput, calls=%fused_computation.8.clone.1 | convolution fusion | flops 541327360 | bytes 1318917 | tf_op jit(solution)/shard_map/while/body/eval_jaxpr/dot_general | solution.py:101
  84.3 4.5 %fusion.59 = f32[64,2048]{1,0:T(8,128)S(1)} fusion(s32[2048]{0:T(1024)S(1)} %dynamic_slice.39, f32[64,2048]{1,0:T(8,128)S(1)} %get-tuple-element.165, bf16[64,40960]{1,0:T(8,128)(2,1)} %get-tuple-element.174, s32[]{:T(128)S(6)} %select_n.263, pred[]{:T(512)S(6)} %compare.34), kind=kOutput, calls=%fused_computation.8.clone.1 | convolution fusion | flops 541327360 | bytes 1318917 | tf_op jit(solution)/shard_map/while/body/eval_jaxpr/dot_general | solution.py:101
  88.8 4.5 %fusion.59 = f32[64,2048]{1,0:T(8,128)S(1)} fusion(s32[2048]{0:T(1024)S(1)} %dynamic_slice.39, f32[64,2048]{1,0:T(8,128)S(1)} %get-tuple-element.165, bf16[64,40960]{1,0:T(8,128)(2,1)} %get-tuple-element.174, s32[]{:T(128)S(6)} %select_n.263, pred[]{:T(512)S(6)} %compare.34), kind=kOutput, calls=%fused_computation.8.clone.1 | convolution fusion | flops 541327360 | bytes 1318917 | tf_op jit(solution)/shard_map/while/body/eval_jaxpr/dot_general | solution.py:101
  93.3 4.5 %fusion.59 = f32[64,2048]{1,0:T(8,128)S(1)} fusion(s32[2048]{0:T(1024)S(1)} %dynamic_slice.39, f32[64,2048]{1,0:T(8,128)S(1)} %get-tuple-element.165, bf16[64,40960]{1,0:T(8,128)(2,1)} %get-tuple-element.174, s32[]{:T(128)S(6)} %select_n.263, pred[]{:T(512)S(6)} %compare.34), kind=kOutput, calls=%fused_computation.8.clone.1 | convolution fusion | flops 541327360 | bytes 1318917 | tf_op jit(solution)/shard_map/while/body/eval_jaxpr/dot_general | solution.py:101
  97.9 4.5 %fusion.59 = f32[64,2048]{1,0:T(8,128)S(1)} fusion(s32[2048]{0:T(1024)S(1)} %dynamic_slice.39, f32[64,2048]{1,0:T(8,128)S(1)} %get-tuple-element.165, bf16[64,40960]{1,0:T(8,128)(2,1)} %get-tuple-element.174, s32[]{:T(128)S(6)} %select_n.263, pred[]{:T(512)S(6)} %compare.34), kind=kOutput, calls=%fused_computation.8.clone.1 | convolution fusion | flops 541327360 | bytes 1318917 | tf_op jit(solution)/shard_map/while/body/eval_jaxpr/dot_general | solution.py:101
  102.4 4.5 %fusion.59 = f32[64,2048]{1,0:T(8,128)S(1)} fusion(s32[2048]{0:T(1024)S(1)} %dynamic_slice.39, f32[64,2048]{1,0:T(8,128)S(1)} %get-tuple-element.165, bf16[64,40960]{1,0:T(8,128)(2,1)} %get-tuple-element.174, s32[]{:T(128)S(6)} %select_n.263, pred[]{:T(512)S(6)} %compare.34), kind=kOutput, calls=%fused_computation.8.clone.1 | convolution fusion | flops 541327360 | bytes 1318917 | tf_op jit(solution)/shard_map/while/body/eval_jaxpr/dot_general | solution.py:101
  106.9 4.5 %fusion.59 = f32[64,2048]{1,0:T(8,128)S(1)} fusion(s32[2048]{0:T(1024)S(1)} %dynamic_slice.39, f32[64,2048]{1,0:T(8,128)S(1)} %get-tuple-element.165, bf16[64,40960]{1,0:T(8,128)(2,1)} %get-tuple-element.174, s32[]{:T(128)S(6)} %select_n.263, pred[]{:T(512)S(6)} %compare.34), kind=kOutput, calls=%fused_computation.8.clone.1 | convolution fusion | flops 541327360 | bytes 1318917 | tf_op jit(solution)/shard_map/while/body/eval_jaxpr/dot_general | solution.py:101
  111.4 4.5 %fusion.59 = f32[64,2048]{1,0:T(8,128)S(1)} fusion(s32[2048]{0:T(1024)S(1)} %dynamic_slice.39, f32[64,2048]{1,0:T(8,128)S(1)} %get-tuple-element.165, bf16[64,40960]{1,0:T(8,128)(2,1)} %get-tuple-element.174, s32[]{:T(128)S(6)} %select_n.263, pred[]{:T(512)S(6)} %compare.34), kind=kOutput, calls=%fused_computation.8.clone.1 | convolution fusion | flops 541327360 | bytes 1318917 | tf_op jit(solution)/shard_map/while/body/eval_jaxpr/dot_general | solution.py:101
  116.0 4.5 %fusion.59 = f32[64,2048]{1,0:T(8,128)S(1)} fusion(s32[2048]{0:T(1024)S(1)} %dynamic_slice.39, f32[64,2048]{1,0:T(8,128)S(1)} %get-tuple-element.165, bf16[64,40960]{1,0:T(8,128)(2,1)} %get-tuple-element.174, s32[]{:T(128)S(6)} %select_n.263, pred[]{:T(512)S(6)} %compare.34), kind=kOutput, calls=%fused_computation.8.clone.1 | convolution fusion | flops 541327360 | bytes 1318917 | tf_op jit(solution)/shard_map/while/body/eval_jaxpr/dot_general | solution.py:101
  129.5 4.5 %fusion.59 = f32[64,2048]{1,0:T(8,128)S(1)} fusion(s32[2048]{0:T(1024)S(1)} %dynamic_slice.39, f32[64,2048]{1,0:T(8,128)S(1)} %get-tuple-element.165, bf16[64,40960]{1,0:T(8,128)(2,1)} %get-tuple-element.174, s32[]{:T(128)S(6)} %select_n.263, pred[]{:T(512)S(6)} %compare.34), kind=kOutput, calls=%fused_computation.8.clone.1 | convolution fusion | flops 541327360 | bytes 1318917 | tf_op jit(solution)/shard_map/while/body/eval_jaxpr/dot_general | solution.py:101
  134.0 4.5 %fusion.59 = f32[64,2048]{1,0:T(8,128)S(1)} fusion(s32[2048]{0:T(1024)S(1)} %dynamic_slice.39, f32[64,2048]{1,0:T(8,128)S(1)} %get-tuple-element.165, bf16[64,40960]{1,0:T(8,128)(2,1)} %get-tuple-element.174, s32[]{:T(128)S(6)} %select_n.263, pred[]{:T(512)S(6)} %compare.34), kind=kOutput, calls=%fused_computation.8.clone.1 | convolution fusion | flops 541327360 | bytes 1318917 | tf_op jit(solution)/shard_map/while/body/eval_jaxpr/dot_general | solution.py:101
  147.6 4.5 %fusion.59 = f32[64,2048]{1,0:T(8,128)S(1)} fusion(s32[2048]{0:T(1024)S(1)} %dynamic_slice.39, f32[64,2048]{1,0:T(8,128)S(1)} %get-tuple-element.165, bf16[64,40960]{1,0:T(8,128)(2,1)} %get-tuple-element.174, s32[]{:T(128)S(6)} %select_n.263, pred[]{:T(512)S(6)} %compare.34), kind=kOutput, calls=%fused_computation.8.clone.1 | convolution fusion | flops 541327360 | bytes 1318917 | tf_op jit(solution)/shard_map/while/body/eval_jaxpr/dot_general | solution.py:101
  152.1 4.5 %fusion.59 = f32[64,2048]{1,0:T(8,128)S(1)} fusion(s32[2048]{0:T(1024)S(1)} %dynamic_slice.39, f32[64,2048]{1,0:T(8,128)S(1)} %get-tuple-element.165, bf16[64,40960]{1,0:T(8,128)(2,1)} %get-tuple-element.174, s32[]{:T(128)S(6)} %select_n.263, pred[]{:T(512)S(6)} %compare.34), kind=kOutput, calls=%fused_computation.8.clone.1 | convolution fusion | flops 541327360 | bytes 1318917 | tf_op jit(solution)/shard_map/while/body/eval_jaxpr/dot_general | solution.py:101
  157.7 30.0 %all-reduce.3.cloned.1.call-done = bf16[2,32,2048]{2,1,0:T(8,128)(2,1)} async-done(((bf16[2,32,2048]{2,1,0:T(8,128)(2,1)}), bf16[2,32,2048]{2,1,0:T(8,128)(2,1)}) %all-reduce.3.cloned.1.call-update) | async-done | bytes 262160 | tf_op jit(solution)/shard_map/psum | solution.py:106
  187.7 68.3 %fusion.27 = bf16[2,8,2048]{2,1,0:T(8,128)(2,1)S(1)} fusion(s32[2048]{0:T(1024)S(1)} %add_select_fusion.6, pred[2048]{0:T(1024)(128)(4,1)S(1)} %fusion.36, bf16[2,32,2048]{2,1,0:T(8,128)(2,1)} %all-reduce.3.cloned.1.call-done, s32[]{:T(128)S(6)} %select_n.186), kind=kOutput, calls=%fused_computation.40 | convolution fusion | flops 205619200 | bytes 141316 | tf_op jit(solution)/shard_map/dot_general | solution.py:108
  257.8 12.2 %all_to_all.25 = bf16[8,2,2048]{2,1,0:T(2,128)(2,1)S(1)} all-to-all(bf16[8,2,2048]{2,1,0:T(2,128)(2,1)S(1)} %reshape.314), channel_id=1, replica_groups=mesh['blk'=8,'beam'=4] {'blk'}, dimensions={0} | all-to-all | bytes 131072 | tf_op jit(solution)/shard_map/all_to_all | solution.py:114
  271.5 22.5 %fusion.23 = bf16[128,2,1152]{2,1,0:T(2,128)(2,1)} fusion(bf16[128,8,16,2]{1,3,0,2:T(2,128)(2,1)S(1)} %bitcast.52, bf16[128,8,16,1152]{3,2,1,0:T(8,128)(2,1)} %param.15), kind=kOutput, calls=%fused_computation.38 | convolution fusion | flops 75792384 | bytes 38404096 | tf_op jit(solution)/shard_map/mqtl,mqtp->mpl/dot_general | solution.py:117
  294.0 30.5 %all-reduce.5.cloned.1.call-done = bf16[128,2,1152]{2,1,0:T(2,128)(2,1)} async-done(((bf16[128,2,1152]{2,1,0:T(2,128)(2,1)}), bf16[128,2,1152]{2,1,0:T(2,128)(2,1)}) %all-reduce.5.cloned.1.call-update) | async-done | bytes 589840 | tf_op jit(solution)/shard_map/psum | solution.py:118
  (76 shorter events, 51.9 us)
Async XLA Ops:
  16.1 14.3 %all-to-all-start.1 = ((bf16[8,2,2560]{2,1,0:T(2,128)(2,1)}), bf16[8,2,2560]{2,1,0:T(2,128)(2,1)S(1)}, u32[]{:S(2)}, u32[]{:S(2)}) async-start(bf16[8,2,2560]{2,1,0:T(2,128)(2,1)} %reshape.312), calls=%async_computation.1 | async-start | bytes 163840 | tf_op jit(solution)/shard_map/all_to_all | solution.py:71
  30.5 10.9 %all-to-all-start = ((s32[1,8,5120]{2,0,1:T(1,128)}), s32[1,8,5120]{2,0,1:T(1,128)S(1)}, u32[]{:S(2)}, u32[]{:S(2)}) async-start(s32[1,8,5120]{2,0,1:T(1,128)} %copy.17), calls=%async_computation | async-start | bytes 327680 | tf_op jit(solution)/shard_map/all_to_all | solution.py:78
  33.9 153.8 %all-reduce.3.cloned.1.call-start = ((), (), s32[]{:S(2)}) async-start(), calls=%async_computation.3 | async-start | bytes 524288 | tf_op jit(solution)/shard_map/psum | solution.py:106
  157.4 167.1 %all-reduce.5.cloned.1.call-start = ((), (), s32[]{:S(2)}) async-start(), calls=%async_computation.4 | async-start | bytes 1179648 | tf_op jit(solution)/shard_map/psum | solution.py:118
Sparse Core Ops, SparseCore 0:
  157.5 30.1 all-reduce.2
  294.1 30.3 all-reduce.4
where the time goes:
time: 334 us; the launch traced here: 333 us
  matrix products  180 us (54%)
  waiting for transfers between devices  71.6 us (21%)
  other arithmetic  33 us (10%)
  between operations  13.7 us (4%)
  blocking collectives  12.2 us (4%)
  starting transfers between devices  11.2 us (3%)
  local copies, waits for them, and re-layouts  10.4 us (3%)
    dot_general x20, matrix products, bin_block(): return carry + jnp.dot(part, onehot, preferred_element_type=jnp.float32)  89.4 us
    dot_general x1, matrix products, shards(): jnp.dot(mine.astype(jnp.bfloat16).reshape(CYCLE_DEV * share, NPHI), phi_t...  68.3 us
    psum x1, waiting for transfers between devices, shards(): lax.psum(partial_sum.astype(jnp.bfloat16), 'beam').astype(jnp.float32)  30.5 us
    psum x1, waiting for transfers between devices, shards(): summed = lax.psum(cube.astype(jnp.bfloat16), 'beam').astype(jnp.float32)  30 us
    dot_general x1, matrix products, shards(): jnp.einsum('mqtl,mqtp->mpl', wigner, coeffs, preferred_element_type=jnp.f...  22.5 us
    select_n x1, other arithmetic, shards(): jnp.where(cycle_of[None, :] == level, received, jnp.zeros_like(received))  21.8 us
    all_to_all x1, blocking collectives, shards(): lax.all_to_all(spectra, 'blk', split_axis=2, concat_axis=0, tiled=True)  12.2 us
    all_to_all x1, starting transfers between devices, shards(): lax.all_to_all(arrange(sample_value[None, :]).astype(jnp.bfloat16), 'blk'...  7.31 us
  transfers between devices with their start and end apart: 4, of which 4 were waited for; matrix products, arithmetic and copies ran while one was open for 1% of the time, Pallas kernels for 0%

commit v1 on v0

--- a/solution.py
+++ b/solution.py
@@ -40,6 +40,11 @@
 
 
 def shards(signal, weight, cycle, phi, psi, owner, wigner):
+
+    def turns_fix(packet):
+        u_next = jax.lax.all_gather(packet, "beam")
+        return jnp.sum(u_next, axis=0)
+
     groups = lax.axis_size("blk")
     beams = lax.axis_size("beam")
     blocks = owner.shape[0]
@@ -103,7 +108,7 @@
     cube = lax.fori_loop(0, turns, bin_block, jnp.zeros((CYCLE_DEV * NPSI, NPHI), jnp.float32))
     cube = cube.reshape(CYCLE_DEV, NPSI, NPHI)
     share = NPSI // beams
-    summed = lax.psum(cube.astype(jnp.bfloat16), "beam").astype(jnp.float32)
+    summed = turns_fix(cube.astype(jnp.bfloat16)).astype(jnp.float32)
     mine = lax.dynamic_slice_in_dim(summed, lax.axis_index("beam") * share, share, 1)
     spectra = jnp.dot(
         mine.astype(jnp.bfloat16).reshape(CYCLE_DEV * share, NPHI),

time: 334 us -> 319 us (0.955)
  waiting for transfers between devices: 71.6 us -> 56 us
    psum x1 -> x0, waiting for transfers between devices: 30 us -> none  [shards(): summed = lax.psum(cube.astype(jnp.bfloat16), 'beam').astype(jnp.float32)]
    all_gather x0 -> x1, waiting for transfers between devices: none -> 14.4 us  [turns_fix(): u_next = jax.lax.all_gather(packet, 'beam')]
where the time goes in v1:
time: 319 us; the launch traced here: 318 us
  matrix products  179 us (56%)
  waiting for transfers between devices  56 us (18%)
  other arithmetic  34.4 us (11%)
  between operations  13.7 us (4%)
  blocking collectives  12.2 us (4%)
  starting transfers between devices  11.2 us (4%)
  local copies, waits for them, and re-layouts  10.4 us (3%)
    dot_general x20, matrix products, bin_block(): return carry + jnp.dot(part, onehot, preferred_element_type=jnp.float32)  89.5 us
    dot_general x1, matrix products, shards(): jnp.dot(mine.astype(jnp.bfloat16).reshape(CYCLE_DEV * share, NPHI), phi_t...  67.5 us
    psum x1, waiting for transfers between devices, shards(): lax.psum(partial_sum.astype(jnp.bfloat16), 'beam').astype(jnp.float32)  30.6 us
    dot_general x1, matrix products, shards(): jnp.einsum('mqtl,mqtp->mpl', wigner, coeffs, preferred_element_type=jnp.f...  22.5 us
    select_n x1, other arithmetic, shards(): jnp.where(cycle_of[None, :] == level, received, jnp.zeros_like(received))  21.8 us
    all_gather x1, waiting for transfers between devices, turns_fix(): u_next = jax.lax.all_gather(packet, 'beam')  14.4 us
    all_to_all x1, blocking collectives, shards(): lax.all_to_all(spectra, 'blk', split_axis=2, concat_axis=0, tiled=True)  12.2 us
    all_to_all x1, starting transfers between devices, shards(): lax.all_to_all(arrange(sample_value[None, :]).astype(jnp.bfloat16), 'blk'...  7.31 us
  transfers between devices with their start and end apart: 4, of which 4 were waited for; matrix products, arithmetic and copies ran while one was open for 1% of the time, Pallas kernels for 0%

profile of v1, /device:TPU:0, one launch (start us, length us, event | category | flops | bytes accessed | tf_op | source)
XLA Modules:
  0.0 318.1 jit_solution(14300442300268046084)
XLA Ops:
  16.1 7.3 %all-to-all-start.1 = ((bf16[8,2,2560]{2,1,0:T(2,128)(2,1)}), bf16[8,2,2560]{2,1,0:T(2,128)(2,1)S(1)}, u32[]{:S(2)}, u32[]{:S(2)}) async-start(bf16[8,2,2560]{2,1,0:T(2,128)(2,1)} %reshape.322), calls=%async_computation.1 | async-start | bytes 163840 | tf_op jit(solution)/shard_map/all_to_all | solution.py:76
  34.4 7.0 %all-to-all-done = s32[1,8,5120]{2,0,1:T(1,128)S(1)} async-done(((s32[1,8,5120]{2,0,1:T(1,128)}), s32[1,8,5120]{2,0,1:T(1,128)S(1)}, u32[]{:S(2)}, u32[]{:S(2)}) %all-to-all-start) | async-done | bytes 163872 | tf_op jit(solution)/shard_map/all_to_all | solution.py:83
  41.7 21.8 %broadcast_select_fusion.1 = (bf16[32,40960]{1,0:T(8,128)(2,1)S(1)}, bf16[32,40960]{1,0:T(8,128)(2,1)S(1)}) fusion(pred[40960]{0:T(1024)(128)(4,1)S(1)} %get-tuple-element.129, f32[40960]{0:T(1024)S(1)} %bitcast.53, s32[40960]{0:T(1024)S(1)} %get-tuple-element.128, s32[32]{0:T(128)S(1)} %add_select_fusion.8, pred[32]{0:T(512)(128)(4,1)S(1)} %iota_compare_fusion.5, ...), kind=kLoop, calls=%fused_computation.37 | loop fusion | flops 24903680 | bytes 5652640 | tf_op jit(solution)/shard_map/jit(_where)/select_n | solution.py:92
  66.2 90.4 %while.14 = (s32[]{:T(128)}, f32[64,2048]{1,0:T(8,128)S(1)}, bf16[64,40960]{1,0:T(8,128)(2,1)}, s32[40960]{0:T(1024)S(1)}, s32[]{:T(128)}, /*index=5*/s32[]{:T(128)}, s32[]{:T(128)}, s32[]{:T(128)}) while((s32[]{:T(128)}, f32[64,2048]{1,0:T(8,128)S(1)}, bf16[64,40960]{1,0:T(8,128)(2,1)}, s32[40960]{0:T(1024)S(1)}, s32[]{:T(128)}, ...), condition=%wide.region_5.6_spmd.clone, body=%wide.region_4.5_spmd.clone.sunk | while | flops 541327360 | bytes 1335445 | solution.py:108
  70.7 4.5 %fusion.59 = f32[64,2048]{1,0:T(8,128)S(1)} fusion(s32[2048]{0:T(1024)S(1)} %dynamic_slice.39, f32[64,2048]{1,0:T(8,128)S(1)} %get-tuple-element.165, bf16[64,40960]{1,0:T(8,128)(2,1)} %get-tuple-element.174, s32[]{:T(128)S(6)} %select_n.263, pred[]{:T(512)S(6)} %compare.34), kind=kOutput, calls=%fused_computation.8.clone.1 | convolution fusion | flops 541327360 | bytes 1318917 | tf_op jit(solution)/shard_map/while/body/eval_jaxpr/dot_general | solution.py:106
  75.3 4.5 %fusion.59 = f32[64,2048]{1,0:T(8,128)S(1)} fusion(s32[2048]{0:T(1024)S(1)} %dynamic_slice.39, f32[64,2048]{1,0:T(8,128)S(1)} %get-tuple-element.165, bf16[64,40960]{1,0:T(8,128)(2,1)} %get-tuple-element.174, s32[]{:T(128)S(6)} %select_n.263, pred[]{:T(512)S(6)} %compare.34), kind=kOutput, calls=%fused_computation.8.clone.1 | convolution fusion | flops 541327360 | bytes 1318917 | tf_op jit(solution)/shard_map/while/body/eval_jaxpr/dot_general | solution.py:106
  79.8 4.5 %fusion.59 = f32[64,2048]{1,0:T(8,128)S(1)} fusion(s32[2048]{0:T(1024)S(1)} %dynamic_slice.39, f32[64,2048]{1,0:T(8,128)S(1)} %get-tuple-element.165, bf16[64,40960]{1,0:T(8,128)(2,1)} %get-tuple-element.174, s32[]{:T(128)S(6)} %select_n.263, pred[]{:T(512)S(6)} %compare.34), kind=kOutput, calls=%fused_computation.8.clone.1 | convolution fusion | flops 541327360 | bytes 1318917 | tf_op jit(solution)/shard_map/while/body/eval_jaxpr/dot_general | solution.py:106
  84.3 4.5 %fusion.59 = f32[64,2048]{1,0:T(8,128)S(1)} fusion(s32[2048]{0:T(1024)S(1)} %dynamic_slice.39, f32[64,2048]{1,0:T(8,128)S(1)} %get-tuple-element.165, bf16[64,40960]{1,0:T(8,128)(2,1)} %get-tuple-element.174, s32[]{:T(128)S(6)} %select_n.263, pred[]{:T(512)S(6)} %compare.34), kind=kOutput, calls=%fused_computation.8.clone.1 | convolution fusion | flops 541327360 | bytes 1318917 | tf_op jit(solution)/shard_map/while/body/eval_jaxpr/dot_general | solution.py:106
  88.8 4.5 %fusion.59 = f32[64,2048]{1,0:T(8,128)S(1)} fusion(s32[2048]{0:T(1024)S(1)} %dynamic_slice.39, f32[64,2048]{1,0:T(8,128)S(1)} %get-tuple-element.165, bf16[64,40960]{1,0:T(8,128)(2,1)} %get-tuple-element.174, s32[]{:T(128)S(6)} %select_n.263, pred[]{:T(512)S(6)} %compare.34), kind=kOutput, calls=%fused_computation.8.clone.1 | convolution fusion | flops 541327360 | bytes 1318917 | tf_op jit(solution)/shard_map/while/body/eval_jaxpr/dot_general | solution.py:106
  93.3 4.5 %fusion.59 = f32[64,2048]{1,0:T(8,128)S(1)} fusion(s32[2048]{0:T(1024)S(1)} %dynamic_slice.39, f32[64,2048]{1,0:T(8,128)S(1)} %get-tuple-element.165, bf16[64,40960]{1,0:T(8,128)(2,1)} %get-tuple-element.174, s32[]{:T(128)S(6)} %select_n.263, pred[]{:T(512)S(6)} %compare.34), kind=kOutput, calls=%fused_computation.8.clone.1 | convolution fusion | flops 541327360 | bytes 1318917 | tf_op jit(solution)/shard_map/while/body/eval_jaxpr/dot_general | solution.py:106
  97.9 4.5 %fusion.59 = f32[64,2048]{1,0:T(8,128)S(1)} fusion(s32[2048]{0:T(1024)S(1)} %dynamic_slice.39, f32[64,2048]{1,0:T(8,128)S(1)} %get-tuple-element.165, bf16[64,40960]{1,0:T(8,128)(2,1)} %get-tuple-element.174, s32[]{:T(128)S(6)} %select_n.263, pred[]{:T(512)S(6)} %compare.34), kind=kOutput, calls=%fused_computation.8.clone.1 | convolution fusion | flops 541327360 | bytes 1318917 | tf_op jit(solution)/shard_map/while/body/eval_jaxpr/dot_general | solution.py:106
  102.4 4.5 %fusion.59 = f32[64,2048]{1,0:T(8,128)S(1)} fusion(s32[2048]{0:T(1024)S(1)} %dynamic_slice.39, f32[64,2048]{1,0:T(8,128)S(1)} %get-tuple-element.165, bf16[64,40960]{1,0:T(8,128)(2,1)} %get-tuple-element.174, s32[]{:T(128)S(6)} %select_n.263, pred[]{:T(512)S(6)} %compare.34), kind=kOutput, calls=%fused_computation.8.clone.1 | convolution fusion | flops 541327360 | bytes 1318917 | tf_op jit(solution)/shard_map/while/body/eval_jaxpr/dot_general | solution.py:106
  106.9 4.5 %fusion.59 = f32[64,2048]{1,0:T(8,128)S(1)} fusion(s32[2048]{0:T(1024)S(1)} %dynamic_slice.39, f32[64,2048]{1,0:T(8,128)S(1)} %get-tuple-element.165, bf16[64,40960]{1,0:T(8,128)(2,1)} %get-tuple-element.174, s32[]{:T(128)S(6)} %select_n.263, pred[]{:T(512)S(6)} %compare.34), kind=kOutput, calls=%fused_computation.8.clone.1 | convolution fusion | flops 541327360 | bytes 1318917 | tf_op jit(solution)/shard_map/while/body/eval_jaxpr/dot_general | solution.py:106
  111.4 4.5 %fusion.59 = f32[64,2048]{1,0:T(8,128)S(1)} fusion(s32[2048]{0:T(1024)S(1)} %dynamic_slice.39, f32[64,2048]{1,0:T(8,128)S(1)} %get-tuple-element.165, bf16[64,40960]{1,0:T(8,128)(2,1)} %get-tuple-element.174, s32[]{:T(128)S(6)} %select_n.263, pred[]{:T(512)S(6)} %compare.34), kind=kOutput, calls=%fused_computation.8.clone.1 | convolution fusion | flops 541327360 | bytes 1318917 | tf_op jit(solution)/shard_map/while/body/eval_jaxpr/dot_general | solution.py:106
  116.0 4.5 %fusion.59 = f32[64,2048]{1,0:T(8,128)S(1)} fusion(s32[2048]{0:T(1024)S(1)} %dynamic_slice.39, f32[64,2048]{1,0:T(8,128)S(1)} %get-tuple-element.165, bf16[64,40960]{1,0:T(8,128)(2,1)} %get-tuple-element.174, s32[]{:T(128)S(6)} %select_n.263, pred[]{:T(512)S(6)} %compare.34), kind=kOutput, calls=%fused_computation.8.clone.1 | convolution fusion | flops 541327360 | bytes 1318917 | tf_op jit(solution)/shard_map/while/body/eval_jaxpr/dot_general | solution.py:106
  129.5 4.5 %fusion.59 = f32[64,2048]{1,0:T(8,128)S(1)} fusion(s32[2048]{0:T(1024)S(1)} %dynamic_slice.39, f32[64,2048]{1,0:T(8,128)S(1)} %get-tuple-element.165, bf16[64,40960]{1,0:T(8,128)(2,1)} %get-tuple-element.174, s32[]{:T(128)S(6)} %select_n.263, pred[]{:T(512)S(6)} %compare.34), kind=kOutput, calls=%fused_computation.8.clone.1 | convolution fusion | flops 541327360 | bytes 1318917 | tf_op jit(solution)/shard_map/while/body/eval_jaxpr/dot_general | solution.py:106
  134.0 4.5 %fusion.59 = f32[64,2048]{1,0:T(8,128)S(1)} fusion(s32[2048]{0:T(1024)S(1)} %dynamic_slice.39, f32[64,2048]{1,0:T(8,128)S(1)} %get-tuple-element.165, bf16[64,40960]{1,0:T(8,128)(2,1)} %get-tuple-element.174, s32[]{:T(128)S(6)} %select_n.263, pred[]{:T(512)S(6)} %compare.34), kind=kOutput, calls=%fused_computation.8.clone.1 | convolution fusion | flops 541327360 | bytes 1318917 | tf_op jit(solution)/shard_map/while/body/eval_jaxpr/dot_general | solution.py:106
  147.6 4.5 %fusion.59 = f32[64,2048]{1,0:T(8,128)S(1)} fusion(s32[2048]{0:T(1024)S(1)} %dynamic_slice.39, f32[64,2048]{1,0:T(8,128)S(1)} %get-tuple-element.165, bf16[64,40960]{1,0:T(8,128)(2,1)} %get-tuple-element.174, s32[]{:T(128)S(6)} %select_n.263, pred[]{:T(512)S(6)} %compare.34), kind=kOutput, calls=%fused_computation.8.clone.1 | convolution fusion | flops 541327360 | bytes 1318917 | tf_op jit(solution)/shard_map/while/body/eval_jaxpr/dot_general | solution.py:106
  152.1 4.5 %fusion.59 = f32[64,2048]{1,0:T(8,128)S(1)} fusion(s32[2048]{0:T(1024)S(1)} %dynamic_slice.39, f32[64,2048]{1,0:T(8,128)S(1)} %get-tuple-element.165, bf16[64,40960]{1,0:T(8,128)(2,1)} %get-tuple-element.174, s32[]{:T(128)S(6)} %select_n.263, pred[]{:T(512)S(6)} %compare.34), kind=kOutput, calls=%fused_computation.8.clone.1 | convolution fusion | flops 541327360 | bytes 1318917 | tf_op jit(solution)/shard_map/while/body/eval_jaxpr/dot_general | solution.py:106
  157.7 14.4 %all-gather.2.cloned.1.call-done = bf16[4,2,32,2048]{3,2,1,0:T(8,128)(2,1)} async-done(((bf16[1,2,32,2048]{3,2,1,0:T(8,128)(2,1)}), bf16[4,2,32,2048]{3,2,1,0:T(8,128)(2,1)}) %all-gather.2.cloned.1.call-update) | async-done | bytes 1048592 | tf_op jit(solution)/shard_map/all_gather | solution.py:45
  173.5 67.5 %fusion.27 = bf16[2,8,2048]{2,1,0:T(8,128)(2,1)S(1)} fusion(s32[2048]{0:T(1024)S(1)} %add_select_fusion.6, pred[2048]{0:T(1024)(128)(4,1)S(1)} %fusion.36, bf16[2,32,2048]{2,1,0:T(8,128)(2,1)S(1)} %reduce_sum.25, s32[]{:T(128)S(6)} %select_n.186), kind=kOutput, calls=%fused_computation.40 | convolution fusion | flops 205619200 | bytes 141316 | tf_op jit(solution)/shard_map/dot_general | solution.py:113
  242.8 12.2 %all_to_all.25 = bf16[8,2,2048]{2,1,0:T(2,128)(2,1)S(1)} all-to-all(bf16[8,2,2048]{2,1,0:T(2,128)(2,1)S(1)} %reshape.324), channel_id=1, replica_groups=mesh['blk'=8,'beam'=4] {'blk'}, dimensions={0} | all-to-all | bytes 131072 | tf_op jit(solution)/shard_map/all_to_all | solution.py:119
  256.5 22.5 %fusion.23 = bf16[128,2,1152]{2,1,0:T(2,128)(2,1)} fusion(bf16[128,8,16,2]{1,3,0,2:T(2,128)(2,1)S(1)} %bitcast.52, bf16[128,8,16,1152]{3,2,1,0:T(8,128)(2,1)} %param.15), kind=kOutput, calls=%fused_computation.38 | convolution fusion | flops 75792384 | bytes 38404096 | tf_op jit(solution)/shard_map/mqtl,mqtp->mpl/dot_general | solution.py:122
  279.0 30.6 %all-reduce.2.cloned.1.call-done = bf16[128,2,1152]{2,1,0:T(2,128)(2,1)} async-done(((bf16[128,2,1152]{2,1,0:T(2,128)(2,1)}), bf16[128,2,1152]{2,1,0:T(2,128)(2,1)}) %all-reduce.2.cloned.1.call-update) | async-done | bytes 589840 | tf_op jit(solution)/shard_map/psum | solution.py:123
  (77 shorter events, 53.3 us)
Async XLA Ops:
  16.1 14.3 %all-to-all-start.1 = ((bf16[8,2,2560]{2,1,0:T(2,128)(2,1)}), bf16[8,2,2560]{2,1,0:T(2,128)(2,1)S(1)}, u32[]{:S(2)}, u32[]{:S(2)}) async-start(bf16[8,2,2560]{2,1,0:T(2,128)(2,1)} %reshape.322), calls=%async_computation.1 | async-start | bytes 163840 | tf_op jit(solution)/shard_map/all_to_all | solution.py:76
  30.5 10.9 %all-to-all-start = ((s32[1,8,5120]{2,0,1:T(1,128)}), s32[1,8,5120]{2,0,1:T(1,128)S(1)}, u32[]{:S(2)}, u32[]{:S(2)}) async-start(s32[1,8,5120]{2,0,1:T(1,128)} %copy.17), calls=%async_computation | async-start | bytes 327680 | tf_op jit(solution)/shard_map/all_to_all | solution.py:83
  33.9 138.2 %all-gather.2.cloned.1.call-start = ((), (), s32[]{:S(2)}) async-start(), calls=%async_computation.3 | async-start | bytes 1310720 | tf_op jit(solution)/shard_map/all_gather | solution.py:45
  157.4 152.2 %all-reduce.2.cloned.1.call-start = ((), (), s32[]{:S(2)}) async-start(), calls=%async_computation.4 | async-start | bytes 1179648 | tf_op jit(solution)/shard_map/psum | solution.py:123
Sparse Core Ops, SparseCore 0:
  157.5 14.5 all-gather.1
  279.1 30.3 all-reduce.1
